TPU v7x, 256 devices: a whole 4x4x8 slice. The times are simulated.
256 devices in a mesh: depth: 64 (over x, z, core), strip: 4 (over y).
Axes of the slice: x: 4, y: 4, z: 8, core: 2. Of those that a mesh axis runs over, the one named last changes fastest.
Arguments:
- density: bfloat16 [256, 64, 1024], P('depth', 'strip'), may hold values from -6 to 6
- tf_bins: int32 [256, 64, 1024], P('depth', 'strip'), may hold values from 0 to 15
- tf_table: float32 [4, 16], replicated, may hold values from 0.2 to 2
- brick_order: int32 [4, 64], P('strip'), may hold values from 0 to 63, each once within a row
Outputs:
- image: float32 [4, 65536], P(None, ('strip', 'depth'))
Inputs may be any that keep to these rules, and one draw needn't show every extreme that they name: `tf_bins`: each voxel's bin indexes a column of tf_table. `brick_order`: each row lists every brick once.
All inputs are finite; a program needn't handle non-finite values.
Results may differ from a plain program's by a relative error of at most 0.0017.
Values may be sent and summed in bfloat16 or wider, within the bound.
A program may use at most 64 MiB of HBM per device.

v0:
```python
import jax
import jax.numpy as jnp
from jax import lax
from jax.sharding import PartitionSpec as P

LIGHT_X = 0.36
LIGHT_Y = 0.48
LIGHT_Z = 0.8
SHADE_GAIN = 1.5


def with_halo(cells, sides, width):
    for axis, dim in sides:
        count = lax.axis_size(axis)
        ends = count - 1
        head = lax.slice_in_dim(cells, 0, width, axis=dim)
        tail = lax.slice_in_dim(cells, cells.shape[dim] - width, cells.shape[dim], axis=dim)
        cells = jnp.concatenate(
            [
                lax.ppermute(tail, axis, [(i, (i + 1) % count) for i in range(ends)]),
                cells,
                lax.ppermute(head, axis, [((i + 1) % count, i) for i in range(ends)]),
            ],
            axis=dim,
        )
    return cells


def shear_plane(values, plane_index):
    across = values.shape[-1]
    offset = 3 * plane_index // 8
    fraction = (3 * plane_index % 8).astype(jnp.float32) / 8.0
    columns = jnp.arange(across, dtype=jnp.int32)
    first = jnp.where(columns < across - offset, jnp.roll(values, -offset, axis=2), 0.0)
    second = jnp.where(columns < across - offset - 1, jnp.roll(first, -1, axis=2), 0.0)
    return (1.0 - fraction) * first + fraction * second


def plane_terms(window, tf_plane, tf_table, plane_index, total_planes):
    beneath = window[0]
    middle = window[1]
    overhead = window[2]
    centre = middle[1:-1]
    sideways = jnp.pad(centre, ((0, 0), (1, 1)))
    slope_across = 0.5 * (sideways[:, 2:] - sideways[:, :-2])
    slope_down = 0.5 * (middle[2:] - middle[:-2])
    slope_deep = 0.5 * (overhead[1:-1] - beneath[1:-1])
    lengths = jnp.sqrt(
        1.0 + slope_across * slope_across + slope_down * slope_down + slope_deep * slope_deep
    )
    shading = (LIGHT_X * slope_across + LIGHT_Y * slope_down + LIGHT_Z * slope_deep) / lengths
    classes = jnp.arange(tf_table.shape[1], dtype=jnp.int32)
    onehot = (tf_plane[None, :, :] == classes[:, None, None]).astype(jnp.float32)
    looked = jnp.einsum("cm,myx->cyx", tf_table, onehot, precision=lax.Precision.HIGHEST)
    extinction = looked[0] * (1.0 + centre * centre) / total_planes
    opacity = 1.0 - jnp.exp(-extinction)
    emitted = looked[1:] * (opacity * jnp.exp(SHADE_GAIN * shading))[None]
    return shear_plane(jnp.concatenate([extinction[None], emitted], axis=0), plane_index)


def order_mask(sequence):
    bricks = sequence.shape[0]
    slots = jnp.arange(bricks, dtype=jnp.int32)
    onehot = (sequence[:, None] == slots[None, :]).astype(jnp.int32)
    position = jnp.sum(onehot * slots[:, None], axis=0)
    return (position[None, :] < position[:, None]).astype(jnp.float32)


def per_device(density, tf_bins, tf_table, brick_order):
    planes = density.shape[0]
    height = density.shape[1]
    across = density.shape[2]
    bricks = lax.axis_size("depth")
    block = with_halo(density, (("depth", 0), ("strip", 1)), 1)
    first_plane = lax.axis_index("depth") * planes
    total_planes = planes * bricks
    colour = jnp.zeros((3, height, across), jnp.float32)
    depth_sum = jnp.zeros((height, across), jnp.float32)
    for plane_at in range(planes):
        window = block[plane_at : plane_at + 3].astype(jnp.float32)
        sheared = plane_terms(
            window, tf_bins[plane_at], tf_table, first_plane + plane_at, total_planes
        )
        colour = colour + jnp.exp(-depth_sum)[None] * sheared[1:]
        depth_sum = depth_sum + sheared[0]
    pixels = height * across
    before = order_mask(brick_order[0])
    flat_colour = colour.reshape(3, pixels)
    flat_depth = depth_sum.reshape(1, pixels)
    partial_value = jnp.concatenate([flat_colour, flat_depth], axis=0)[:, None, :]
    received = lax.all_to_all(
        partial_value.astype(jnp.bfloat16), "depth", split_axis=2, concat_axis=1, tiled=True
    ).astype(partial_value.dtype)
    depths = received[3]
    prefix = jnp.dot(before, depths, precision=lax.Precision.HIGHEST)
    weight = jnp.exp(-prefix)
    shown = jnp.sum(weight[None] * received[:3], axis=1)
    remaining = jnp.exp(-jnp.sum(depths, axis=0))
    return jnp.concatenate([shown, remaining[None]], axis=0)


def solution(mesh):
    in_specs = (P("depth", "strip", None), P("depth", "strip", None), P(), P("strip", None))
    out_specs = P(None, ("strip", "depth"))
    return jax.shard_map(
        per_device, mesh=mesh, in_specs=in_specs, out_specs=out_specs, check_vma=False
    )
```

profile of v0, /device:TPU:1, one launch (start us, length us, event | category | flops | bytes accessed | tf_op | source)
XLA Modules:
  0.0 676.8 jit_solution(5689342530783288285)
XLA Ops:
  0.0 0.8 fusion.84
  0.8 4.9 collective-permute-start
  5.7 1.9 collective-permute-start.1
  7.7 1.0 slice_bitcast_fusion.1
  10.5 0.9 constant_dynamic-update-slice_fusion.1
  11.5 3.2 collective-permute-start.2
  14.7 1.3 collective-permute-start.3
  16.6 2.6 collective-permute-done.3
  19.9 0.7 fusion.21
  21.7 0.7 fusion.9
  23.2 0.7 fusion.27
  24.6 0.7 fusion.31
  26.0 13.2 %copy.98 = bf16[4,1,16384]{0,1,2:T(2,128)(2,1)} copy(bf16[4,1,16384]{2,0,1:T(4,128)(2,1)S(1)} %pad_maximum_fusion.2) | data formatting | bytes 262144 | tf_op jit(solution)/shard_map/concatenate | solution.py:90
  39.7 90.8 %reduce.6 = bf16[16384,4]{1,0:T(8,128)(2,1)} reduce(bf16[16384,1,4]{2,1,0:T(2,128)(2,1)} %bitcast.201, bf16[]{:T(256)} %broadcast.130), dimensions={1}, to_apply=%bitcast.190.reduce_sub_computation | reduce | bytes 262146
  130.4 9.3 %reshape.196 = bf16[64,2,512]{2,1,0:T(2,128)(2,1)} reshape(bf16[16384,4]{1,0:T(8,128)(2,1)} %reduce.6) | data formatting | bytes 262144
  139.8 14.3 %all-to-all-start = ((bf16[64,2,512]{2,1,0:T(2,128)(2,1)}), bf16[64,2,512]{2,1,0:T(2,128)(2,1)S(1)}, u32[]{:S(2)}, u32[]{:S(2)}) async-start(bf16[64,2,512]{2,1,0:T(2,128)(2,1)} %reshape.196), calls=%async_computation | async-start | bytes 262144 | tf_op jit(solution)/shard_map/all_to_all | solution.py:91
  154.2 10.2 %all-to-all-done = bf16[64,2,512]{2,1,0:T(2,128)(2,1)S(1)} async-done(((bf16[64,2,512]{2,1,0:T(2,128)(2,1)}), bf16[64,2,512]{2,1,0:T(2,128)(2,1)S(1)}, u32[]{:S(2)}, u32[]{:S(2)}) %all-to-all-start) | async-done | bytes 131104 | tf_op jit(solution)/shard_map/all_to_all | solution.py:91
  164.4 17.1 %reshape.197 = bf16[16384,1,4]{2,1,0:T(2,128)(2,1)} reshape(bf16[64,2,512]{2,1,0:T(2,128)(2,1)S(1)} %all-to-all-done) | data formatting | bytes 262144
  181.5 11.0 %slice.394 = f32[3,1,16384]{0,1,2:T(1,128)} slice(bf16[4,1,16384]{0,1,2:T(2,128)(2,1)} %bitcast.199), slice={[0:3], [0:1], [0:16384]} | slice | bytes 393216 | tf_op jit(solution)/shard_map/slice | solution.py:97
  192.6 233.5 %slice_reduce_fusion.1 = bf16[16384]{0:T(1024)(128)(2,1)S(1)} fusion(bf16[4,1,16384]{0,1,2:T(2,128)(2,1)S(1)} %bitcast.200), kind=kLoop, calls=%fused_computation.1 | loop fusion | bytes 65536 | tf_op jit(solution)/shard_map/slice | solution.py:94
  426.0 9.9 %bitcast_convert_fusion = f32[4,1,16384]{0,1,2:T(1,128)} fusion(bf16[16384,1,4]{2,1,0:T(2,128)(2,1)S(1)} %copy-done.1), kind=kLoop, calls=%fused_computation.204 | loop fusion | flops 65536 | bytes 393216 | tf_op jit(solution)/shard_map/convert_element_type | solution.py:93
  435.9 5.2 copy.100
  441.1 234.7 %slice_reduce_fusion = f32[16384]{0:T(1024)S(1)} fusion(f32[4,1,16384]{0,1,2:T(1,128)} %bitcast_convert_fusion), kind=kLoop, calls=%fused_computation | loop fusion | bytes 131072 | tf_op jit(solution)/shard_map/slice | solution.py:94
  676.2 0.6 pad_maximum_fusion.3
  (73 shorter events, 7.0 us)
Async XLA Ops:
  0.0 8.7 %copy-start = (f32[4,16]{1,0:T(4,128)S(1)}, f32[4,16]{1,0:T(4,128)}, u32[]{:S(2)}) copy-start(f32[4,16]{1,0:T(4,128)} %param.8) | copy-start | bytes 772
  0.8 9.7 %collective-permute-start = (bf16[1,16,1024]{2,1,0:T(8,128)(2,1)S(1)}, bf16[1,16,1024]{2,1,0:T(8,128)(2,1)S(1)}, u32[]{:S(2)}, u32[]{:S(2)}) collective-permute-start(bf16[1,16,1024]{2,1,0:T(8,128)(2,1)S(1)} %get-tuple-element.32), channel_id=1, source_target_pairs={{0,4},{4,8},{8,12},{12,16},{16,20},{20,24},{24,28},{28,32},{32,36}... | collective-permute-start | bytes 98312 | tf_op jit(solution)/shard_map/ppermute | solution.py:20
  5.7 5.7 collective-permute-start.1
  11.5 5.2 collective-permute-start.2
  14.7 4.6 collective-permute-start.3
  39.7 114.4 %copy-start.2 = (s32[1,64]{1,0:T(1,128)S(1)}, s32[1,64]{1,0:T(1,128)}, u32[]{:S(2)}) copy-start(s32[1,64]{1,0:T(1,128)} %param.9) | copy-start | bytes 772
  139.8 24.7 %all-to-all-start = ((bf16[64,2,512]{2,1,0:T(2,128)(2,1)}), bf16[64,2,512]{2,1,0:T(2,128)(2,1)S(1)}, u32[]{:S(2)}, u32[]{:S(2)}) async-start(bf16[64,2,512]{2,1,0:T(2,128)(2,1)} %reshape.196), calls=%async_computation | async-start | bytes 262144 | tf_op jit(solution)/shard_map/all_to_all | solution.py:91
  181.5 11.0 %copy-start.1 = (bf16[16384,1,4]{2,1,0:T(2,128)(2,1)S(1)}, bf16[16384,1,4]{2,1,0:T(2,128)(2,1)}, u32[]{:S(2)}) copy-start(bf16[16384,1,4]{2,1,0:T(2,128)(2,1)} %reshape.197) | copy-start | bytes 393220
where the time goes:
time: 677 us
  local copies, waits for them, and re-layouts  529 us (78%)
  other arithmetic  107 us (16%)
  starting transfers between devices  25.7 us (4%)
  waiting for transfers between devices  12.8 us (2%)
    slice x3, local copies, waits for them, and re-layouts, per_device(): depths = received[3]  468 us
    unnamed x1, other arithmetic  90.8 us
    unnamed x14, local copies, waits for them, and re-layouts  27.9 us
    slice x2, local copies, waits for them, and re-layouts, per_device(): shown = jnp.sum(weight[None] * received[:3], axis=1)  16.2 us
    all_to_all x1, starting transfers between devices, per_device(): lax.all_to_all(partial_value.astype(jnp.bfloat16), 'depth', split_axis=2,...  14.3 us
  transfers between devices with their start and end apart: 5, of which 2 were waited for; matrix products, arithmetic and copies ran while one was open for 1% of the time, Pallas kernels for 0%

commit v1 on v0

v1 whole, which is shorter than its diff:
```python
import functools

import jax
import jax.numpy as jnp
from jax import lax
from jax.experimental import pallas as pl
from jax.experimental.pallas import tpu as pltpu
from jax.sharding import PartitionSpec as P

LIGHT_X = 0.36
LIGHT_Y = 0.48
LIGHT_Z = 0.8
SHADE_GAIN = 1.5
MESH = pl.DeviceIdType.MESH
LANES = 128
SUB = 8
F32 = jnp.float32


def kernel(
    bricks, strips, planes, height, across, classes,
    dens_hbm, bins_hbm, table_hbm, order_hbm, out_ref,
    dens_v, bins_v, table_v, order_s, tab, field, rows_out, rows_in, plane_in,
    part_a, part_q, near, far, depth, wide, packed, arrived,
    in_sem, halo_send, halo_recv, tile_send, tile_recv,
):
    me = lax.axis_index("depth")
    strip = lax.axis_index("strip")
    tiles = across // LANES
    halves = height // SUB
    per_owner = height * tiles // bricks
    rows_msg = 4 * per_owner

    barrier = pltpu.get_barrier_semaphore()

    def greet(step, carry):
        pl.semaphore_signal(
            barrier, inc=1, device_id={"depth": lax.rem(me + step, bricks)}, device_id_type=MESH
        )
        return carry

    lax.fori_loop(1, bricks, greet, 0)

    @pl.when(strip > 0)
    def _():
        pl.semaphore_signal(barrier, inc=1, device_id={"strip": strip - 1}, device_id_type=MESH)

    @pl.when(strip < strips - 1)
    def _():
        pl.semaphore_signal(barrier, inc=1, device_id={"strip": strip + 1}, device_id_type=MESH)

    loads = [
        pltpu.make_async_copy(dens_hbm, dens_v, in_sem.at[0]),
        pltpu.make_async_copy(bins_hbm, bins_v, in_sem.at[1]),
        pltpu.make_async_copy(table_hbm, table_v, in_sem.at[2]),
        pltpu.make_async_copy(order_hbm, order_s, in_sem.at[3]),
    ]
    for load in loads:
        load.start()

    loads[0].wait()
    for p in range(planes):
        for t in range(tiles):
            field[p + 1, t, SUB : SUB + height, :] = dens_v[
                p, :, t * LANES : (t + 1) * LANES
            ].astype(F32)
    for p in range(planes):
        for t in range(tiles):
            rows_out[0, p, t : t + 1, :] = field[p + 1, t, SUB : SUB + 1, :]
            rows_out[1, p, t : t + 1, :] = field[p + 1, t, SUB + height - 1 : SUB + height, :]
    loads[2].wait()
    tab[0:4, 0:classes] = table_v[...]
    loads[1].wait()

    lane = lax.broadcasted_iota(jnp.int32, (SUB, LANES), 1)
    zero = jnp.zeros((SUB, LANES), F32)
    columns = [jnp.broadcast_to(tab[c : c + 1, :], (SUB, LANES)) for c in range(4)]
    depth[...] = jnp.zeros_like(depth)

    def shear_of(p):
        scaled = 3 * (me * planes + p)
        offset = scaled // 8
        fraction = (scaled % 8).astype(F32) * 0.125
        return offset, fraction

    def plane_terms(p, carry):
        offset, fraction = shear_of(p)
        roll_a = lax.rem(LANES - offset, LANES)
        roll_b = LANES - 1 - offset
        mask_a = lane < LANES - offset
        mask_b = lane < LANES - 1 - offset
        for h in range(halves):
            rows = slice(SUB + SUB * h, 2 * SUB + SUB * h)
            before = [(zero, zero)] * 4
            for t in reversed(range(tiles)):
                centre = field[p + 1, t, rows, :]
                right = field[p + 1, t + 1, rows, :] if t < tiles - 1 else zero
                left = field[p + 1, t - 1, rows, :] if t > 0 else zero
                up = jnp.where(lane < LANES - 1, pltpu.roll(centre, LANES - 1, 1), pltpu.roll(right, LANES - 1, 1))
                down = jnp.where(lane > 0, pltpu.roll(centre, 1, 1), pltpu.roll(left, 1, 1))
                slope = 0.5 * (up - down)
                part_a[h, p, t] = LIGHT_X * slope
                part_q[h, p, t] = 1.0 + slope * slope
                spot = bins_v[p, SUB * h : SUB * h + SUB, t * LANES : (t + 1) * LANES]
                looked = [
                    jnp.take_along_axis(column, spot, axis=1, mode="promise_in_bounds")
                    for column in columns
                ]
                extinction = looked[0] * (1.0 + centre * centre) * (1.0 / (planes * bricks))
                opacity = 1.0 - jnp.exp(-extinction)
                fields = [extinction] + [entry * opacity for entry in looked[1:]]
                rolled = [(pltpu.roll(v, roll_a, 1), pltpu.roll(v, roll_b, 1)) for v in fields]
                first = [jnp.where(mask_a, rolled[i][0], before[i][0]) for i in range(4)]
                second = [jnp.where(mask_b, rolled[i][1], before[i][1]) for i in range(4)]
                before = rolled
                sofar = depth[h, t]
                through = jnp.exp(-sofar)
                depth[h, t] = sofar + ((1.0 - fraction) * first[0] + fraction * second[0])
                scale_a = (1.0 - fraction) * through
                scale_b = fraction * through
                for c in range(3):
                    near[c, h, p, t] = scale_a * first[c + 1]
                    far[c, h, p, t] = scale_b * second[c + 1]
        return carry

    lax.fori_loop(0, planes, plane_terms, 0)

    has_below = me > 0
    has_over = me < bricks - 1
    has_upper = strip > 0
    has_lower = strip < strips - 1
    greeted = bricks - 1 + has_upper.astype(jnp.int32) + has_lower.astype(jnp.int32)
    pl.semaphore_wait(barrier, greeted)

    def halo(src, dst, slot, target):
        return pltpu.make_async_remote_copy(
            src_ref=src, dst_ref=dst, send_sem=halo_send.at[slot], recv_sem=halo_recv.at[slot],
            device_id=target, device_id_type=MESH,
        )

    to_over = halo(dens_v.at[planes - 1], plane_in.at[0], 0, {"depth": lax.rem(me + 1, bricks)})
    to_below = halo(dens_v.at[0], plane_in.at[1], 1, {"depth": lax.rem(me + bricks - 1, bricks)})
    to_lower = halo(rows_out.at[1], rows_in.at[0], 2, {"strip": lax.rem(strip + 1, strips)})
    to_upper = halo(rows_out.at[0], rows_in.at[1], 3, {"strip": lax.rem(strip + strips - 1, strips)})

    pl.when(has_over)(to_over.start)
    pl.when(has_below)(to_below.start)
    pl.when(has_lower)(to_lower.start)
    pl.when(has_upper)(to_upper.start)

    @pl.when(has_below)
    def _():
        to_over.wait_recv()
        for t in range(tiles):
            field[0, t, SUB : SUB + height, :] = plane_in[0, :, t * LANES : (t + 1) * LANES].astype(F32)

    @pl.when(jnp.logical_not(has_below))
    def _():
        for t in range(tiles):
            field[0, t, SUB : SUB + height, :] = jnp.zeros((height, LANES), F32)

    @pl.when(has_over)
    def _():
        to_below.wait_recv()
        for t in range(tiles):
            field[planes + 1, t, SUB : SUB + height, :] = plane_in[1, :, t * LANES : (t + 1) * LANES].astype(F32)

    @pl.when(jnp.logical_not(has_over))
    def _():
        for t in range(tiles):
            field[planes + 1, t, SUB : SUB + height, :] = jnp.zeros((height, LANES), F32)

    @pl.when(has_upper)
    def _():
        to_lower.wait_recv()
        for p in range(planes):
            for t in range(tiles):
                field[p + 1, t, SUB - 1 : SUB, :] = rows_in[0, p, t : t + 1, :]

    @pl.when(jnp.logical_not(has_upper))
    def _():
        for p in range(planes):
            for t in range(tiles):
                field[p + 1, t, SUB - 1 : SUB, :] = jnp.zeros((1, LANES), F32)

    @pl.when(has_lower)
    def _():
        to_upper.wait_recv()
        for p in range(planes):
            for t in range(tiles):
                field[p + 1, t, SUB + height : SUB + height + 1, :] = rows_in[1, p, t : t + 1, :]

    @pl.when(jnp.logical_not(has_lower))
    def _():
        for p in range(planes):
            for t in range(tiles):
                field[p + 1, t, SUB + height : SUB + height + 1, :] = jnp.zeros((1, LANES), F32)

    def tile_copy(owner):
        return pltpu.make_async_remote_copy(
            src_ref=packed.at[owner], dst_ref=arrived.at[me], send_sem=tile_send, recv_sem=tile_recv,
            device_id={"depth": owner}, device_id_type=MESH,
        )

    shears = [shear_of(p) for p in range(planes)]
    owners = bricks // halves
    for h in range(halves):
        rows = slice(SUB + SUB * h, 2 * SUB + SUB * h)
        above = slice(SUB + SUB * h - 1, 2 * SUB + SUB * h - 1)
        under = slice(SUB + SUB * h + 1, 2 * SUB + SUB * h + 1)
        before = [(zero, zero)] * planes
        for t in reversed(range(tiles)):
            colour = [zero] * 3
            for p in range(planes):
                offset = shears[p][0]
                slope_down = 0.5 * (field[p + 1, t, under, :] - field[p + 1, t, above, :])
                slope_deep = 0.5 * (field[p + 2, t, rows, :] - field[p, t, rows, :])
                square = part_q[h, p, t] + slope_down * slope_down + slope_deep * slope_deep
                toward = part_a[h, p, t] + LIGHT_Y * slope_down + LIGHT_Z * slope_deep
                gain = jnp.exp(SHADE_GAIN * toward * lax.rsqrt(square))
                gain_a = pltpu.roll(gain, lax.rem(LANES - offset, LANES), 1)
                gain_b = pltpu.roll(gain, LANES - 1 - offset, 1)
                first = jnp.where(lane < LANES - offset, gain_a, before[p][0])
                second = jnp.where(lane < LANES - 1 - offset, gain_b, before[p][1])
                before[p] = (gain_a, gain_b)
                for c in range(3):
                    colour[c] = colour[c] + (near[c, h, p, t] * first + far[c, h, p, t] * second)
            spot = SUB * h * tiles + t
            start = spot // per_owner * rows_msg + spot % per_owner
            for c, value in enumerate(colour + [depth[h, t]]):
                wide[pl.ds(start + c * per_owner, SUB, stride=tiles * 4), :] = value
        for owner in range(owners * h, owners * (h + 1)):
            packed[owner] = wide[owner * rows_msg : (owner + 1) * rows_msg, :].astype(jnp.bfloat16)

        def send(step, carry, h=h):
            owner = owners * h + lax.rem(me + step, owners)
            pl.when(owner != me)(lambda: tile_copy(owner).start())
            return carry

        lax.fori_loop(0, owners, send, 0)

    arrived[me] = packed[me]
    loads[3].wait()
    pl.when(has_over)(to_over.wait_send)
    pl.when(has_below)(to_below.wait_send)
    pl.when(has_lower)(to_lower.wait_send)
    pl.when(has_upper)(to_upper.wait_send)
    everyone = pltpu.make_async_remote_copy(
        src_ref=packed.at[pl.ds(0, bricks - 1)], dst_ref=arrived.at[pl.ds(0, bricks - 1)],
        send_sem=tile_send, recv_sem=tile_recv,
        device_id={"depth": lax.rem(me + 1, bricks)}, device_id_type=MESH,
    )
    everyone.wait_recv()

    row = lax.broadcasted_iota(jnp.int32, (rows_msg, LANES), 0)
    last = row >= 3 * per_owner

    def layer(slot, carry):
        shown, prefix = carry
        for inner in range(8):
            tile = arrived[order_s[0, slot * 8 + inner]].astype(F32)
            shown = shown + jnp.exp(-prefix) * tile
            spread = jnp.where(last, tile, 0.0)
            spread = spread + pltpu.roll(spread, 2 * per_owner, 0)
            spread = spread + pltpu.roll(spread, per_owner, 0)
            prefix = prefix + spread
        return shown, prefix

    blank = jnp.zeros((rows_msg, LANES), F32)
    shown, prefix = lax.fori_loop(0, bricks // 8, layer, (blank, blank))
    shown = jnp.where(last, jnp.exp(-prefix), shown)
    for r in range(rows_msg):
        c, piece = r // per_owner, r % per_owner
        out_ref[c : c + 1, piece * LANES : (piece + 1) * LANES] = shown[r : r + 1, :]
    everyone.wait_send()


def solution(mesh):
    bricks = mesh.shape["depth"]
    strips = mesh.shape["strip"]

    def per_device(density, tf_bins, tf_table, brick_order):
        planes, height, across = density.shape
        classes = tf_table.shape[1]
        tiles = across // LANES
        halves = height // SUB
        owned = height * across // bricks
        rows_msg = 4 * owned // LANES
        return pl.pallas_call(
            functools.partial(kernel, bricks, strips, planes, height, across, classes),
            out_shape=jax.ShapeDtypeStruct((4, owned), F32),
            in_specs=[pl.BlockSpec(memory_space=pl.ANY)] * 4,
            out_specs=pl.BlockSpec(memory_space=pltpu.VMEM),
            scratch_shapes=[
                pltpu.VMEM((planes, height, across), jnp.bfloat16),
                pltpu.VMEM((planes, height, across), jnp.int32),
                pltpu.VMEM((4, classes), F32),
                pltpu.SMEM((1, bricks), jnp.int32),
                pltpu.VMEM((SUB, LANES), F32),
                pltpu.VMEM((planes + 2, tiles, height + 2 * SUB, LANES), F32),
                pltpu.VMEM((2, planes, tiles, LANES), F32),
                pltpu.VMEM((2, planes, tiles, LANES), F32),
                pltpu.VMEM((2, height, across), jnp.bfloat16),
                pltpu.VMEM((halves, planes, tiles, SUB, LANES), F32),
                pltpu.VMEM((halves, planes, tiles, SUB, LANES), F32),
                pltpu.VMEM((3, halves, planes, tiles, SUB, LANES), F32),
                pltpu.VMEM((3, halves, planes, tiles, SUB, LANES), F32),
                pltpu.VMEM((halves, tiles, SUB, LANES), F32),
                pltpu.VMEM((bricks * rows_msg, LANES), F32),
                pltpu.VMEM((bricks, rows_msg, LANES), jnp.bfloat16),
                pltpu.VMEM((bricks, rows_msg, LANES), jnp.bfloat16),
                pltpu.SemaphoreType.DMA((4,)),
                pltpu.SemaphoreType.DMA((4,)),
                pltpu.SemaphoreType.DMA((4,)),
                pltpu.SemaphoreType.DMA,
                pltpu.SemaphoreType.DMA,
            ],
            compiler_params=pltpu.CompilerParams(collective_id=0, has_side_effects=True),
        )(density, tf_bins, tf_table, brick_order)

    return jax.shard_map(
        per_device,
        mesh=mesh,
        in_specs=(P("depth", "strip", None), P("depth", "strip", None), P(), P("strip", None)),
        out_specs=P(None, ("strip", "depth")),
        check_vma=False,
    )
```

time: 677 us -> 24.6 us (0.04)
  local copies, waits for them, and re-layouts: 529 us -> 1.28 us
  other arithmetic: 107 us -> 0 us
  starting transfers between devices: 25.7 us -> 0 us
  Pallas kernels: 0 us -> 23.2 us
  waiting for transfers between devices: 12.8 us -> 0 us
    slice x19 -> x0, local copies, waits for them, and re-layouts: 486 us -> none  [the longest x3 468 us: per_device(): depths = received[3]]
    unnamed x1 -> x0, other arithmetic: 90.8 us -> none
    unnamed x14 -> x1, local copies, waits for them, and re-layouts: 27.9 us -> 1.28 us
    pallas_call x0 -> x1, Pallas kernels: none -> 23.2 us  [per_device(): pl.pallas_call(functools.partial(kernel, bricks, strips, planes, height,...]
    all_to_all x1 -> x0, starting transfers between devices: 14.3 us -> none  [per_device(): lax.all_to_all(partial_value.astype(jnp.bfloat16), 'depth', split_axis=2,...]
    concatenate x2 -> x0, local copies, waits for them, and re-layouts: 13.2 us -> none  [the longest x1 13.2 us: per_device(): jnp.concatenate([flat_colour, flat_depth], axis=0)[:, None, :]]
    ppermute x4 -> x0, starting transfers between devices: 11.3 us -> none  [the longest x2 8.11 us: with_halo(): lax.ppermute(tail, axis, [(i, (i + 1) % count) for i in range(ends)])]
    all_to_all x1 -> x0, waiting for transfers between devices: 10.2 us -> none  [per_device(): lax.all_to_all(partial_value.astype(jnp.bfloat16), 'depth', split_axis=2,...]
  transfers between devices with their start and end apart: 5 -> 0, of which waited for: 2 -> 0; matrix products, arithmetic and copies ran while one was open for 1% -> 0% of each run, Pallas kernels for 0% -> 0%
where the time goes in v1:
time: 24.6 us; the launch traced here: 24.4 us
  Pallas kernels  23.2 us (94%)
  local copies, waits for them, and re-layouts  1.28 us (5%)
    pallas_call x1, Pallas kernels, per_device(): pl.pallas_call(functools.partial(kernel, bricks, strips, planes, height,...  23.2 us
    unnamed x1, local copies, waits for them, and re-layouts  1.28 us

profile of v1, /device:TPU:1, one launch (start us, length us, event | category | flops | bytes accessed | tf_op | source)
XLA Modules:
  0.0 24.4 jit_solution(8854298316399890967)
XLA Ops:
  0.0 23.2 %shard_map.46 = f32[4,256]{1,0:T(4,128)} custom-call(bf16[4,16,1024]{2,1,0:T(8,128)(2,1)} %dens_hbm.1, s32[4,16,1024]{2,1,0:T(8,128)} %bins_hbm.1, f32[4,16]{1,0:T(4,128)} %table_hbm.1, s32[1,64]{1,0:T(1,128)} %order_hbm.1), custom_call_target="tpu_custom_call" | custom-call | tf_op jit(solution)/shard_map/pallas_call | solution.py:289
  23.2 1.3 %copy.6 = f32[4,256]{1,0:T(4,128)} copy(f32[4,256]{1,0:T(4,128)} %shard_map.46) | data formatting | bytes 8192

commit v2 on v1

--- a/solution.py
+++ b/solution.py
@@ -13,6 +13,7 @@
 SHADE_GAIN = 1.5
 MESH = pl.DeviceIdType.MESH
 LANES = 128
+RING = 8
 SUB = 8
 F32 = jnp.float32
 
@@ -21,8 +22,8 @@
     bricks, strips, planes, height, across, classes,
     dens_hbm, bins_hbm, table_hbm, order_hbm, out_ref,
     dens_v, bins_v, table_v, order_s, tab, field, rows_out, rows_in, plane_in,
-    part_a, part_q, near, far, depth, wide, packed, arrived,
-    in_sem, halo_send, halo_recv, tile_send, tile_recv,
+    raw, part_a, part_q, near, far, depth, wide, packed, arrived,
+    in_sem, halo_send, halo_recv, tile_send, tile_recv, late_in, all_in,
 ):
     me = lax.axis_index("depth")
     strip = lax.axis_index("strip")
@@ -31,23 +32,76 @@
     per_owner = height * tiles // bricks
     rows_msg = 4 * per_owner
 
+    cores = 2
+    deep = min(RING, bricks // cores)
+    rows_x = bricks // (cores * deep)
+    core = me % cores
+    z = me // cores % deep
+    x = me // (cores * deep)
+    half = deep // 2
+    late = z >= half
+    early = jnp.logical_not(late)
+    has_below = me > 0
+    has_over = me < bricks - 1
+    has_upper = strip > 0
+    has_lower = strip < strips - 1
+    below = lax.rem(me + bricks - 1, bricks)
+    over = lax.rem(me + 1, bricks)
+
+    def place(x_to, z_to, core_to):
+        return (x_to * deep + z_to) * cores + core_to
+
+    def is_late(index):
+        return index // cores % deep >= half
+
+    def signal(sem, target):
+        pl.semaphore_signal(sem, inc=1, device_id=target, device_id_type=MESH)
+
     barrier = pltpu.get_barrier_semaphore()
 
-    def greet(step, carry):
-        pl.semaphore_signal(
-            barrier, inc=1, device_id={"depth": lax.rem(me + step, bricks)}, device_id_type=MESH
+    @pl.when(has_upper)
+    def _():
+        signal(barrier, {"strip": strip - 1})
+
+    @pl.when(has_lower)
+    def _():
+        signal(barrier, {"strip": strip + 1})
+
+    @pl.when(jnp.logical_and(late, has_below))
+    def _():
+        signal(barrier, {"depth": below})
+
+    @pl.when(jnp.logical_and(late, has_over))
+    def _():
+        signal(barrier, {"depth": over})
+
+    @pl.when(early)
+    def _():
+        def greet(step, carry):
+            signal(barrier, {"depth": lax.rem(me + step, bricks)})
+            return carry
+
+        lax.fori_loop(1, bricks, greet, 0)
+
+    greeted = (
+        bricks // 2
+        - early.astype(jnp.int32)
+        + has_upper.astype(jnp.int32)
+        + has_lower.astype(jnp.int32)
+        + jnp.logical_and(has_below, is_late(below)).astype(jnp.int32)
+        + jnp.logical_and(has_over, is_late(over)).astype(jnp.int32)
+    )
+
+    def halo(src, dst, slot, target):
+        return pltpu.make_async_remote_copy(
+            src_ref=src, dst_ref=dst, send_sem=halo_send.at[slot], recv_sem=halo_recv.at[slot],
+            device_id=target, device_id_type=MESH,
         )
-        return carry
-
-    lax.fori_loop(1, bricks, greet, 0)
-
-    @pl.when(strip > 0)
-    def _():
-        pl.semaphore_signal(barrier, inc=1, device_id={"strip": strip - 1}, device_id_type=MESH)
-
-    @pl.when(strip < strips - 1)
-    def _():
-        pl.semaphore_signal(barrier, inc=1, device_id={"strip": strip + 1}, device_id_type=MESH)
+
+    to_over = halo(dens_hbm.at[planes - 1], plane_in.at[0], 0, {"depth": over})
+    to_below = halo(dens_hbm.at[0], plane_in.at[1], 1, {"depth": below})
+    to_lower = halo(rows_out.at[1], rows_in.at[0], 2, {"strip": lax.rem(strip + 1, strips)})
+    to_upper = halo(rows_out.at[0], rows_in.at[1], 3, {"strip": lax.rem(strip + strips - 1, strips)})
 
     loads = [
         pltpu.make_async_copy(dens_hbm, dens_v, in_sem.at[0]),
@@ -58,6 +112,10 @@
     for load in loads:
         load.start()
 
+    pl.semaphore_wait(barrier, greeted)
+    pl.when(has_over)(to_over.start)
+    pl.when(has_below)(to_below.start)
+
     loads[0].wait()
     for p in range(planes):
         for t in range(tiles):
@@ -68,6 +126,17 @@
         for t in range(tiles):
             rows_out[0, p, t : t + 1, :] = field[p + 1, t, SUB : SUB + 1, :]
             rows_out[1, p, t : t + 1, :] = field[p + 1, t, SUB + height - 1 : SUB + height, :]
+    pl.when(has_lower)(to_lower.start)
+    pl.when(has_upper)(to_upper.start)
+
+    @pl.when(late)
+    def _():
+        def report(step, carry):
+            signal(late_in, {"depth": place(step // (half * cores), step // cores % half, step % cores)})
+            return carry
+
+        lax.fori_loop(0, bricks // 2, report, 0)
+
     loads[2].wait()
     tab[0:4, 0:classes] = table_v[...]
     loads[1].wait()
@@ -82,6 +151,25 @@
         offset = scaled // 8
         fraction = (scaled % 8).astype(F32) * 0.125
         return offset, fraction
+
+    def look_up(p, carry):
+        for h in range(halves):
+            rows = slice(SUB + SUB * h, 2 * SUB + SUB * h)
+            for t in range(tiles):
+                centre = field[p + 1, t, rows, :]
+                spot = bins_v[p, SUB * h : SUB * h + SUB, t * LANES : (t + 1) * LANES]
+                looked = [
+                    jnp.take_along_axis(column, spot, axis=1, mode="promise_in_bounds")
+                    for column in columns
+                ]
+                extinction = looked[0] * (1.0 + centre * centre) * (1.0 / (planes * bricks))
+                opacity = 1.0 - jnp.exp(-extinction)
+                raw[0, h, p, t] = extinction
+                for c in range(3):
+                    raw[c + 1, h, p, t] = looked[c + 1] * opacity
+        return carry
+
+    lax.fori_loop(0, planes, look_up, 0)
 
     def plane_terms(p, carry):
         offset, fraction = shear_of(p)
@@ -101,14 +189,7 @@
                 slope = 0.5 * (up - down)
                 part_a[h, p, t] = LIGHT_X * slope
                 part_q[h, p, t] = 1.0 + slope * slope
-                spot = bins_v[p, SUB * h : SUB * h + SUB, t * LANES : (t + 1) * LANES]
-                looked = [
-                    jnp.take_along_axis(column, spot, axis=1, mode="promise_in_bounds")
-                    for column in columns
-                ]
-                extinction = looked[0] * (1.0 + centre * centre) * (1.0 / (planes * bricks))
-                opacity = 1.0 - jnp.exp(-extinction)
-                fields = [extinction] + [entry * opacity for entry in looked[1:]]
+                fields = [raw[c, h, p, t] for c in range(4)]
                 rolled = [(pltpu.roll(v, roll_a, 1), pltpu.roll(v, roll_b, 1)) for v in fields]
                 first = [jnp.where(mask_a, rolled[i][0], before[i][0]) for i in range(4)]
                 second = [jnp.where(mask_b, rolled[i][1], before[i][1]) for i in range(4)]
@@ -125,29 +206,6 @@
 
     lax.fori_loop(0, planes, plane_terms, 0)
 
-    has_below = me > 0
-    has_over = me < bricks - 1
-    has_upper = strip > 0
-    has_lower = strip < strips - 1
-    greeted = bricks - 1 + has_upper.astype(jnp.int32) + has_lower.astype(jnp.int32)
-    pl.semaphore_wait(barrier, greeted)
-
-    def halo(src, dst, slot, target):
-        return pltpu.make_async_remote_copy(
-            src_ref=src, dst_ref=dst, send_sem=halo_send.at[slot], recv_sem=halo_recv.at[slot],
-            device_id=target, device_id_type=MESH,
-        )
-
-    to_over = halo(dens_v.at[planes - 1], plane_in.at[0], 0, {"depth": lax.rem(me + 1, bricks)})
-    to_below = halo(dens_v.at[0], plane_in.at[1], 1, {"depth": lax.rem(me + bricks - 1, bricks)})
-    to_lower = halo(rows_out.at[1], rows_in.at[0], 2, {"strip": lax.rem(strip + 1, strips)})
-    to_upper = halo(rows_out.at[0], rows_in.at[1], 3, {"strip": lax.rem(strip + strips - 1, strips)})
-
-    pl.when(has_over)(to_over.start)
-    pl.when(has_below)(to_below.start)
-    pl.when(has_lower)(to_lower.start)
-    pl.when(has_upper)(to_upper.start)
-
     @pl.when(has_below)
     def _():
         to_over.wait_recv()
@@ -202,8 +260,17 @@
             device_id={"depth": owner}, device_id_type=MESH,
         )
 
+    def send(z_to, carry):
+        for step in range(rows_x):
+            for core_to in range(cores):
+                owner = place(lax.rem(x + step, rows_x), z_to, core_to)
+                if step == 0:
+                    pl.when(owner != me)(lambda owner=owner: tile_copy(owner).start())
+                else:
+                    tile_copy(owner).start()
+        return carry
+
     shears = [shear_of(p) for p in range(planes)]
-    owners = bricks // halves
     for h in range(halves):
         rows = slice(SUB + SUB * h, 2 * SUB + SUB * h)
         above = slice(SUB + SUB * h - 1, 2 * SUB + SUB * h - 1)
@@ -229,15 +296,31 @@
             start = spot // per_owner * rows_msg + spot % per_owner
             for c, value in enumerate(colour + [depth[h, t]]):
                 wide[pl.ds(start + c * per_owner, SUB, stride=tiles * 4), :] = value
-        for owner in range(owners * h, owners * (h + 1)):
-            packed[owner] = wide[owner * rows_msg : (owner + 1) * rows_msg, :].astype(jnp.bfloat16)
-
-        def send(step, carry, h=h):
-            owner = owners * h + lax.rem(me + step, owners)
-            pl.when(owner != me)(lambda: tile_copy(owner).start())
-            return carry
-
-        lax.fori_loop(0, owners, send, 0)
+
+    for owner in range(bricks):
+        packed[owner] = wide[owner * rows_msg : (owner + 1) * rows_msg, :].astype(jnp.bfloat16)
+
+    lax.fori_loop(0, half, send, 0)
+
+    @pl.when(early)
+    def _():
+        pl.semaphore_wait(late_in, bricks // 2)
+
+        @pl.when(z == 0)
+        def _():
+            signal(all_in, {"depth": place(x, deep - 1, core)})
+            signal(all_in, {"depth": place(x, deep - 2, core)})
+
+        @pl.when(z == half - 1)
+        def _():
+            signal(all_in, {"depth": place(x, half, core)})
+            signal(all_in, {"depth": place(x, half + 1, core)})
+
+    @pl.when(late)
+    def _():
+        pl.semaphore_wait(all_in, 1)
+
+    lax.fori_loop(half, deep, send, 0)
 
     arrived[me] = packed[me]
     loads[3].wait()
@@ -301,6 +384,7 @@
                 pltpu.VMEM((2, planes, tiles, LANES), F32),
                 pltpu.VMEM((2, planes, tiles, LANES), F32),
                 pltpu.VMEM((2, height, across), jnp.bfloat16),
+                pltpu.VMEM((4, halves, planes, tiles, SUB, LANES), F32),
                 pltpu.VMEM((halves, planes, tiles, SUB, LANES), F32),
                 pltpu.VMEM((halves, planes, tiles, SUB, LANES), F32),
                 pltpu.VMEM((3, halves, planes, tiles, SUB, LANES), F32),
@@ -314,6 +398,8 @@
                 pltpu.SemaphoreType.DMA((4,)),
                 pltpu.SemaphoreType.DMA,
                 pltpu.SemaphoreType.DMA,
+                pltpu.SemaphoreType.REGULAR,
+                pltpu.SemaphoreType.REGULAR,
             ],
             compiler_params=pltpu.CompilerParams(collective_id=0, has_side_effects=True),
         )(density, tf_bins, tf_table, brick_order)

time: 24.6 us -> 21.2 us (0.86)
  Pallas kernels: 23.2 us -> 19.8 us
    pallas_call x1, Pallas kernels: 23.2 us -> 19.8 us  [per_device(): pl.pallas_call(functools.partial(kernel, bricks, strips, planes, height,...]
where the time goes in v2:
time: 21.2 us; the launch traced here: 21.1 us
  Pallas kernels  19.8 us (93%)
  local copies, waits for them, and re-layouts  1.28 us (6%)
    pallas_call x1, Pallas kernels, per_device(): pl.pallas_call(functools.partial(kernel, bricks, strips, planes, height,...  19.8 us
    unnamed x1, local copies, waits for them, and re-layouts  1.28 us

profile of v2, /device:TPU:1, one launch (start us, length us, event | category | flops | bytes accessed | tf_op | source)
XLA Modules:
  0.0 21.1 jit_solution(17284969099675312184)
XLA Ops:
  0.0 19.8 %shard_map.46 = f32[4,256]{1,0:T(4,128)} custom-call(bf16[4,16,1024]{2,1,0:T(8,128)(2,1)} %dens_hbm.1, s32[4,16,1024]{2,1,0:T(8,128)} %bins_hbm.1, f32[4,16]{1,0:T(4,128)} %table_hbm.1, s32[1,64]{1,0:T(1,128)} %order_hbm.1), custom_call_target="tpu_custom_call" | custom-call | tf_op jit(solution)/shard_map/pallas_call | solution.py:372
  19.8 1.3 %copy.6 = f32[4,256]{1,0:T(4,128)} copy(f32[4,256]{1,0:T(4,128)} %shard_map.46) | data formatting | bytes 8192

commit v3 on v2

v3 whole, which is shorter than its diff:
```python
import functools

import jax
import jax.numpy as jnp
from jax import lax
from jax.experimental import pallas as pl
from jax.experimental.pallas import tpu as pltpu
from jax.sharding import PartitionSpec as P

LIGHT_X = 0.36
LIGHT_Y = 0.48
LIGHT_Z = 0.8
SHADE_GAIN = 1.5
MESH = pl.DeviceIdType.MESH
LANES = 128
RING = 8
EARLY = 3
RELAYS = ((0, (7, 6)), (2, (3, 4, 5)))
SUB = 8
F32 = jnp.float32


def kernel(
    bricks, strips, planes, height, across, classes,
    dens_hbm, bins_hbm, table_hbm, arrived,
    dens_v, bins_v, table_v, tab, field, rows_out, rows_in, plane_in,
    raw, part_a, part_q, near, far, depth, wide, packed,
    in_sem, own_sem, halo_send, halo_recv, tile_send, tile_recv, late_in, all_in,
):
    me = lax.axis_index("depth")
    strip = lax.axis_index("strip")
    tiles = across // LANES
    halves = height // SUB
    per_owner = height * tiles // bricks
    rows_msg = 4 * per_owner

    cores = 2
    deep = min(RING, bricks // cores)
    rows_x = bricks // (cores * deep)
    core = me % cores
    z = me // cores % deep
    x = me // (cores * deep)
    late = z >= EARLY
    pitch = height + 2 * SUB
    early = jnp.logical_not(late)
    has_below = me > 0
    has_over = me < bricks - 1
    has_upper = strip > 0
    has_lower = strip < strips - 1
    below = lax.rem(me + bricks - 1, bricks)
    over = lax.rem(me + 1, bricks)

    def place(x_to, z_to, core_to):
        return (x_to * deep + z_to) * cores + core_to

    def is_late(index):
        return index // cores % deep >= EARLY

    def signal(sem, target):
        pl.semaphore_signal(sem, inc=1, device_id=target, device_id_type=MESH)

    def at(p, t, row, count=SUB):
        start = (p * tiles + t) * pitch + SUB + row
        if not isinstance(start, int) and row % SUB == 0:
            start = pl.multiple_of(start, SUB)
        return pl.ds(start, count)

    def put(p, t, value):
        field[at(p, t, 0, height), :] = value

    def row_of(p, row):
        return pl.ds(p * tiles * pitch + SUB + row, tiles, stride=pitch)

    barrier = pltpu.get_barrier_semaphore()

    @pl.when(has_upper)
    def _():
        signal(barrier, {"strip": strip - 1})

    @pl.when(has_lower)
    def _():
        signal(barrier, {"strip": strip + 1})

    @pl.when(jnp.logical_and(late, has_below))
    def _():
        signal(barrier, {"depth": below})

    @pl.when(jnp.logical_and(late, has_over))
    def _():
        signal(barrier, {"depth": over})

    @pl.when(early)
    def _():
        def greet(step, carry):
            signal(barrier, {"depth": lax.rem(me + step, bricks)})
            return carry

        lax.fori_loop(1, bricks, greet, 0)

    greeted = (
        EARLY * rows_x * cores
        - early.astype(jnp.int32)
        + has_upper.astype(jnp.int32)
        + has_lower.astype(jnp.int32)
        + jnp.logical_and(has_below, is_late(below)).astype(jnp.int32)
        + jnp.logical_and(has_over, is_late(over)).astype(jnp.int32)
    )

    def halo(src, dst, slot, target):
        return pltpu.make_async_remote_copy(
            src_ref=src, dst_ref=dst, send_sem=halo_send.at[slot], recv_sem=halo_recv.at[slot],
            device_id=target, device_id_type=MESH,
        )

    to_over = halo(dens_hbm.at[planes - 1], plane_in.at[0], 0, {"depth": over})
    to_below = halo(dens_hbm.at[0], plane_in.at[1], 1, {"depth": below})
    to_lower = halo(rows_out.at[1], rows_in.at[0], 2, {"strip": lax.rem(strip + 1, strips)})
    to_upper = halo(rows_out.at[0], rows_in.at[1], 3, {"strip": lax.rem(strip + strips - 1, strips)})

    loads = [
        pltpu.make_async_copy(dens_hbm, dens_v, in_sem.at[0]),
        pltpu.make_async_copy(bins_hbm, bins_v, in_sem.at[1]),
        pltpu.make_async_copy(table_hbm, table_v, in_sem.at[2]),
    ]
    for load in loads:
        load.start()

    pl.semaphore_wait(barrier, greeted)
    pl.when(has_over)(to_over.start)
    pl.when(has_below)(to_below.start)

    loads[0].wait()
    for p in range(planes):
        for t in range(tiles):
            put(p + 1, t, dens_v[p, :, t * LANES : (t + 1) * LANES].astype(F32))
    for p in range(planes):
        rows_out[0, p] = field[row_of(p + 1, 0), :].astype(jnp.bfloat16)
        rows_out[1, p] = field[row_of(p + 1, height - 1), :].astype(jnp.bfloat16)
    pl.when(has_lower)(to_lower.start)
    pl.when(has_upper)(to_upper.start)

    @pl.when(late)
    def _():
        def report(step, carry):
            signal(late_in, {"depth": place(step // (EARLY * cores), step // cores % EARLY, step % cores)})
            return carry

        lax.fori_loop(0, EARLY * rows_x * cores, report, 0)

    loads[2].wait()
    tab[0:4, 0:classes] = table_v[...]
    loads[1].wait()

    lane = lax.broadcasted_iota(jnp.int32, (SUB, LANES), 1)
    zero = jnp.zeros((SUB, LANES), F32)
    columns = [jnp.broadcast_to(tab[c : c + 1, :], (SUB, LANES)) for c in range(4)]
    depth[...] = jnp.zeros_like(depth)

    def shear_of(p):
        scaled = 3 * (me * planes + p)
        offset = scaled // 8
        fraction = (scaled % 8).astype(F32) * 0.125
        return offset, fraction

    def look_up(p, carry):
        for h in range(halves):
            for t in range(tiles):
                centre = field[at(p + 1, t, SUB * h), :]
                spot = bins_v[p, SUB * h : SUB * h + SUB, t * LANES : (t + 1) * LANES]
                looked = [
                    jnp.take_along_axis(column, spot, axis=1, mode="promise_in_bounds")
                    for column in columns
                ]
                extinction = looked[0] * (1.0 + centre * centre) * (1.0 / (planes * bricks))
                opacity = 1.0 - jnp.exp(-extinction)
                raw[0, h, p, t] = extinction
                for c in range(3):
                    raw[c + 1, h, p, t] = looked[c + 1] * opacity
        return carry

    lax.fori_loop(0, planes, look_up, 0)

    def plane_terms(p, carry):
        offset, fraction = shear_of(p)
        roll_a = lax.rem(LANES - offset, LANES)
        roll_b = LANES - 1 - offset
        mask_a = lane < LANES - offset
        mask_b = lane < LANES - 1 - offset
        for h in range(halves):
            before = [(zero, zero)] * 4
            for t in reversed(range(tiles)):
                centre = field[at(p + 1, t, SUB * h), :]
                right = field[at(p + 1, t + 1, SUB * h), :] if t < tiles - 1 else zero
                left = field[at(p + 1, t - 1, SUB * h), :] if t > 0 else zero
                up = jnp.where(lane < LANES - 1, pltpu.roll(centre, LANES - 1, 1), pltpu.roll(right, LANES - 1, 1))
                down = jnp.where(lane > 0, pltpu.roll(centre, 1, 1), pltpu.roll(left, 1, 1))
                slope = 0.5 * (up - down)
                part_a[h, p, t] = LIGHT_X * slope
                part_q[h, p, t] = 1.0 + slope * slope
                fields = [raw[c, h, p, t] for c in range(4)]
                rolled = [(pltpu.roll(v, roll_a, 1), pltpu.roll(v, roll_b, 1)) for v in fields]
                first = [jnp.where(mask_a, rolled[i][0], before[i][0]) for i in range(4)]
                second = [jnp.where(mask_b, rolled[i][1], before[i][1]) for i in range(4)]
                before = rolled
                sofar = depth[h, t]
                through = jnp.exp(-sofar)
                depth[h, t] = sofar + ((1.0 - fraction) * first[0] + fraction * second[0])
                scale_a = (1.0 - fraction) * through
                scale_b = fraction * through
                for c in range(3):
                    near[c, h, p, t] = scale_a * first[c + 1]
                    far[c, h, p, t] = scale_b * second[c + 1]
        return carry

    lax.fori_loop(0, planes, plane_terms, 0)

    def fill(present, copy, slot, p):
        @pl.when(present)
        def _():
            copy.wait_recv()
            for t in range(tiles):
                put(p, t, plane_in[slot, :, t * LANES : (t + 1) * LANES].astype(F32))

        @pl.when(jnp.logical_not(present))
        def _():
            for t in range(tiles):
                put(p, t, jnp.zeros((height, LANES), F32))

    fill(has_below, to_over, 0, 0)
    fill(has_over, to_below, 1, planes + 1)

    def border(present, copy, slot, row):
        @pl.when(present)
        def _():
            copy.wait_recv()
            for p in range(planes):
                field[row_of(p + 1, row), :] = rows_in[slot, p].astype(F32)

        @pl.when(jnp.logical_not(present))
        def _():
            for p in range(planes):
                field[row_of(p + 1, row), :] = jnp.zeros((tiles, LANES), F32)

    border(has_upper, to_lower, 0, -1)
    border(has_lower, to_upper, 1, height)

    def tile_copy(owner):
        return pltpu.make_async_remote_copy(
            src_ref=packed.at[owner], dst_ref=arrived.at[me], send_sem=tile_send, recv_sem=tile_recv,
            device_id={"depth": owner}, device_id_type=MESH,
        )

    def send(z_to, carry):
        for step in range(rows_x):
            for core_to in range(cores):
                owner = place(lax.rem(x + step, rows_x), z_to, core_to)
                if step == 0:
                    pl.when(owner != me)(lambda owner=owner: tile_copy(owner).start())
                else:
                    tile_copy(owner).start()
        return carry

    shears = [shear_of(p) for p in range(planes)]
    split = tiles // 2 if 4 * per_owner == tiles else 0

    def shade(low, high):
        for h in range(halves):
            before = [(zero, zero)] * planes
            for t in reversed(range(low, min(high + 1, tiles))):
                colour = [zero] * 3
                for p in range(planes):
                    offset = shears[p][0]
                    row = SUB * h
                    slope_down = 0.5 * (field[at(p + 1, t, row + 1), :] - field[at(p + 1, t, row - 1), :])
                    slope_deep = 0.5 * (field[at(p + 2, t, row), :] - field[at(p, t, row), :])
                    square = part_q[h, p, t] + slope_down * slope_down + slope_deep * slope_deep
                    toward = part_a[h, p, t] + LIGHT_Y * slope_down + LIGHT_Z * slope_deep
                    gain = jnp.exp(SHADE_GAIN * toward * lax.rsqrt(square))
                    gain_a = pltpu.roll(gain, lax.rem(LANES - offset, LANES), 1)
                    gain_b = pltpu.roll(gain, LANES - 1 - offset, 1)
                    if t < high:
                        first = jnp.where(lane < LANES - offset, gain_a, before[p][0])
                        second = jnp.where(lane < LANES - 1 - offset, gain_b, before[p][1])
                        for c in range(3):
                            colour[c] = colour[c] + (near[c, h, p, t] * first + far[c, h, p, t] * second)
                    before[p] = (gain_a, gain_b)
                if t < high:
                    spot = SUB * h * tiles + t
                    start = spot // per_owner * rows_msg + spot % per_owner
                    for c, value in enumerate(colour + [depth[h, t]]):
                        wide[pl.ds(start + c * per_owner, SUB, stride=tiles * 4), :] = value
        for owner in range(bricks):
            first_tile = owner * per_owner % tiles
            if low <= first_tile < high:
                packed[owner] = wide[owner * rows_msg : (owner + 1) * rows_msg, :].astype(jnp.bfloat16)

    if split:
        shade(0, split)
        send(0, 0)
        shade(split, tiles)
    else:
        shade(0, tiles)
        send(0, 0)
    lax.fori_loop(1, EARLY, send, 0)

    @pl.when(early)
    def _():
        pl.semaphore_wait(late_in, (deep - EARLY) * rows_x * cores)
        for source, targets in RELAYS:

            @pl.when(z == source)
            def _(targets=targets):
                for target in targets:
                    signal(all_in, {"depth": place(x, target, core)})

    @pl.when(late)
    def _():
        pl.semaphore_wait(all_in, 1)

    lax.fori_loop(EARLY, deep, send, 0)

    own = pltpu.make_async_copy(packed.at[me], arrived.at[me], own_sem)
    own.start()
    own.wait()
    pl.when(has_over)(to_over.wait_send)
    pl.when(has_below)(to_below.wait_send)
    pl.when(has_lower)(to_lower.wait_send)
    pl.when(has_upper)(to_upper.wait_send)
    everyone = pltpu.make_async_remote_copy(
        src_ref=packed.at[pl.ds(0, bricks - 1)], dst_ref=arrived.at[pl.ds(0, bricks - 1)],
        send_sem=tile_send, recv_sem=tile_recv,
        device_id={"depth": lax.rem(me + 1, bricks)}, device_id_type=MESH,
    )
    everyone.wait_recv()

    everyone.wait_send()


def composite(bricks, per_owner, order, arrived, out_ref):
    rows_msg = 4 * per_owner
    row = lax.broadcasted_iota(jnp.int32, (rows_msg, LANES), 0)
    last = row >= 3 * per_owner

    def layer(slot, carry):
        shown, prefix = carry
        for inner in range(8):
            tile = arrived[order[0, slot * 8 + inner]].astype(F32)
            shown = shown + jnp.exp(-prefix) * tile
            spread = jnp.where(last, tile, 0.0)
            spread = spread + pltpu.roll(spread, 2 * per_owner, 0)
            spread = spread + pltpu.roll(spread, per_owner, 0)
            prefix = prefix + spread
        return shown, prefix

    blank = jnp.zeros((rows_msg, LANES), F32)
    shown, prefix = lax.fori_loop(0, bricks // 8, layer, (blank, blank))
    shown = jnp.where(last, jnp.exp(-prefix), shown)
    for r in range(rows_msg):
        c, piece = r // per_owner, r % per_owner
        out_ref[c : c + 1, piece * LANES : (piece + 1) * LANES] = shown[r : r + 1, :]


def solution(mesh):
    bricks = mesh.shape["depth"]
    strips = mesh.shape["strip"]

    def per_device(density, tf_bins, tf_table, brick_order):
        planes, height, across = density.shape
        classes = tf_table.shape[1]
        tiles = across // LANES
        halves = height // SUB
        owned = height * across // bricks
        rows_msg = 4 * owned // LANES
        arrived = pl.pallas_call(
            functools.partial(kernel, bricks, strips, planes, height, across, classes),
            out_shape=jax.ShapeDtypeStruct((bricks, rows_msg, LANES), jnp.bfloat16),
            in_specs=[pl.BlockSpec(memory_space=pl.ANY)] * 3,
            out_specs=pl.BlockSpec(memory_space=pl.ANY),
            scratch_shapes=[
                pltpu.VMEM((planes, height, across), jnp.bfloat16),
                pltpu.VMEM((planes, height, across), jnp.int32),
                pltpu.VMEM((4, classes), F32),
                pltpu.VMEM((SUB, LANES), F32),
                pltpu.VMEM(((planes + 2) * tiles * (height + 2 * SUB), LANES), F32),
                pltpu.VMEM((2, planes, tiles, LANES), jnp.bfloat16),
                pltpu.VMEM((2, planes, tiles, LANES), jnp.bfloat16),
                pltpu.VMEM((2, height, across), jnp.bfloat16),
                pltpu.VMEM((4, halves, planes, tiles, SUB, LANES), F32),
                pltpu.VMEM((halves, planes, tiles, SUB, LANES), F32),
                pltpu.VMEM((halves, planes, tiles, SUB, LANES), F32),
                pltpu.VMEM((3, halves, planes, tiles, SUB, LANES), F32),
                pltpu.VMEM((3, halves, planes, tiles, SUB, LANES), F32),
                pltpu.VMEM((halves, tiles, SUB, LANES), F32),
                pltpu.VMEM((bricks * rows_msg, LANES), F32),
                pltpu.VMEM((bricks, rows_msg, LANES), jnp.bfloat16),
                pltpu.SemaphoreType.DMA((3,)),
                pltpu.SemaphoreType.DMA,
                pltpu.SemaphoreType.DMA((4,)),
                pltpu.SemaphoreType.DMA((4,)),
                pltpu.SemaphoreType.DMA,
                pltpu.SemaphoreType.DMA,
                pltpu.SemaphoreType.REGULAR,
                pltpu.SemaphoreType.REGULAR,
            ],
            compiler_params=pltpu.CompilerParams(collective_id=0, has_side_effects=True),
        )(density, tf_bins, tf_table)
        return pl.pallas_call(
            functools.partial(composite, bricks, rows_msg // 4),
            out_shape=jax.ShapeDtypeStruct((4, owned), F32),
            in_specs=[
                pl.BlockSpec(memory_space=pltpu.SMEM),
                pl.BlockSpec(memory_space=pltpu.VMEM),
            ],
            out_specs=pl.BlockSpec(memory_space=pltpu.VMEM),
        )(brick_order, arrived)

    return jax.shard_map(
        per_device,
        mesh=mesh,
        in_specs=(P("depth", "strip", None), P("depth", "strip", None), P(), P("strip", None)),
        out_specs=P(None, ("strip", "depth")),
        check_vma=False,
    )
```

time: 21.2 us -> 19.9 us (0.939)
  local copies, waits for them, and re-layouts: 1.28 us -> 0 us
    pallas_call x1, Pallas kernels: 19.8 us -> 18 us  [per_device(): pl.pallas_call(functools.partial(kernel, bricks, strips, planes, height,...]
    pallas_call x0 -> x1, Pallas kernels: none -> 1.75 us  [per_device(): pl.pallas_call(functools.partial(composite, bricks, rows_msg // 4), out_s...]
    unnamed x1 -> x0, local copies, waits for them, and re-layouts: 1.28 us -> none
where the time goes in v3:
time: 19.9 us; the launch traced here: 19.8 us
  Pallas kernels  19.8 us (99%)
    pallas_call x1, Pallas kernels, per_device(): pl.pallas_call(functools.partial(kernel, bricks, strips, planes, height,...  18 us
    pallas_call x1, Pallas kernels, per_device(): pl.pallas_call(functools.partial(composite, bricks, rows_msg // 4), out_s...  1.75 us

profile of v3, /device:TPU:1, one launch (start us, length us, event | category | flops | bytes accessed | tf_op | source)
XLA Modules:
  0.0 19.8 jit_solution(14246370411955510779)
XLA Ops:
  0.0 18.0 %shard_map.46.arrived = bf16[64,8,128]{2,1,0:T(8,128)(2,1)} custom-call(bf16[4,16,1024]{2,1,0:T(8,128)(2,1)} %dens_hbm.1, s32[4,16,1024]{2,1,0:T(8,128)} %bins_hbm.1, f32[4,16]{1,0:T(4,128)} %table_hbm.1), custom_call_target="tpu_custom_call" | custom-call | tf_op jit(solution)/shard_map/pallas_call | solution.py:374
  18.0 1.8 %shard_map.47 = f32[4,256]{1,0:T(4,128)} custom-call(s32[1,64]{1,0:T(1,128)} %order.1, bf16[64,8,128]{2,1,0:T(8,128)(2,1)} %shard_map.46.arrived), custom_call_target="tpu_custom_call" | custom-call | tf_op jit(solution)/shard_map/pallas_call | solution.py:407

commit v4 on v3

--- a/solution.py
+++ b/solution.py
@@ -15,7 +15,6 @@
 LANES = 128
 RING = 8
 EARLY = 3
-RELAYS = ((0, (7, 6)), (2, (3, 4, 5)))
 SUB = 8
 F32 = jnp.float32
 
@@ -37,12 +36,10 @@
     cores = 2
     deep = min(RING, bricks // cores)
     rows_x = bricks // (cores * deep)
-    core = me % cores
-    z = me // cores % deep
-    x = me // (cores * deep)
-    late = z >= EARLY
+    core = lax.rem(me, cores)
+    z = lax.rem(lax.div(me, cores), deep)
+    x = lax.div(me, cores * deep)
     pitch = height + 2 * SUB
-    early = jnp.logical_not(late)
     has_below = me > 0
     has_over = me < bricks - 1
     has_upper = strip > 0
@@ -54,7 +51,11 @@
         return (x_to * deep + z_to) * cores + core_to
 
     def is_late(index):
-        return index // cores % deep >= EARLY
+        return lax.rem(lax.div(index, cores), deep) >= EARLY + (index < cores * deep).astype(jnp.int32)
+
+    late = is_late(me)
+    early = jnp.logical_not(late)
+    n_early = (EARLY * rows_x + 1) * cores
 
     def signal(sem, target):
         pl.semaphore_signal(sem, inc=1, device_id=target, device_id_type=MESH)
@@ -71,6 +72,18 @@
     def row_of(p, row):
         return pl.ds(p * tiles * pitch + SUB + row, tiles, stride=pitch)
 
+    loads = [
+        pltpu.make_async_copy(dens_hbm.at[planes - 1], dens_v.at[planes - 1], in_sem.at[0]),
+        pltpu.make_async_copy(dens_hbm.at[0], dens_v.at[0], in_sem.at[1]),
+        pltpu.make_async_copy(
+            dens_hbm.at[pl.ds(1, planes - 2)], dens_v.at[pl.ds(1, planes - 2)], in_sem.at[2]
+        ),
+        pltpu.make_async_copy(bins_hbm, bins_v, in_sem.at[3]),
+        pltpu.make_async_copy(table_hbm, table_v, in_sem.at[4]),
+    ]
+    for load in loads:
+        load.start()
+
     barrier = pltpu.get_barrier_semaphore()
 
     @pl.when(has_upper)
@@ -98,7 +111,7 @@
         lax.fori_loop(1, bricks, greet, 0)
 
     greeted = (
-        EARLY * rows_x * cores
+        n_early
         - early.astype(jnp.int32)
         + has_upper.astype(jnp.int32)
         + has_lower.astype(jnp.int32)
@@ -112,44 +125,47 @@
             device_id=target, device_id_type=MESH,
         )
 
-    to_over = halo(dens_hbm.at[planes - 1], plane_in.at[0], 0, {"depth": over})
-    to_below = halo(dens_hbm.at[0], plane_in.at[1], 1, {"depth": below})
-    to_lower = halo(rows_out.at[1], rows_in.at[0], 2, {"strip": lax.rem(strip + 1, strips)})
-    to_upper = halo(rows_out.at[0], rows_in.at[1], 3, {"strip": lax.rem(strip + strips - 1, strips)})
-
-    loads = [
-        pltpu.make_async_copy(dens_hbm, dens_v, in_sem.at[0]),
-        pltpu.make_async_copy(bins_hbm, bins_v, in_sem.at[1]),
-        pltpu.make_async_copy(table_hbm, table_v, in_sem.at[2]),
+    cut = (tiles // 2 + 1) * LANES
+    pieces = (slice(0, cut), slice(cut, across))
+    to_over = [
+        halo(dens_v.at[planes - 1, :, part], plane_in.at[0, :, part], i, {"depth": over})
+        for i, part in enumerate(pieces)
     ]
-    for load in loads:
-        load.start()
-
-    pl.semaphore_wait(barrier, greeted)
-    pl.when(has_over)(to_over.start)
-    pl.when(has_below)(to_below.start)
+    to_below = [
+        halo(dens_v.at[0, :, part], plane_in.at[1, :, part], 2 + i, {"depth": below})
+        for i, part in enumerate(pieces)
+    ]
+    to_lower = halo(rows_out.at[1], rows_in.at[0], 4, {"strip": lax.rem(strip + 1, strips)})
+    to_upper = halo(rows_out.at[0], rows_in.at[1], 5, {"strip": lax.rem(strip + strips - 1, strips)})
 
     loads[0].wait()
+    loads[1].wait()
+    loads[2].wait()
     for p in range(planes):
         for t in range(tiles):
             put(p + 1, t, dens_v[p, :, t * LANES : (t + 1) * LANES].astype(F32))
     for p in range(planes):
         rows_out[0, p] = field[row_of(p + 1, 0), :].astype(jnp.bfloat16)
         rows_out[1, p] = field[row_of(p + 1, height - 1), :].astype(jnp.bfloat16)
+    pl.semaphore_wait(barrier, greeted)
     pl.when(has_lower)(to_lower.start)
     pl.when(has_upper)(to_upper.start)
+    for piece in range(2):
+        pl.when(has_over)(to_over[piece].start)
+        pl.when(has_below)(to_below[piece].start)
 
     @pl.when(late)
     def _():
         def report(step, carry):
-            signal(late_in, {"depth": place(step // (EARLY * cores), step // cores % EARLY, step % cores)})
+            z_to = lax.div(step, rows_x * cores)
+            signal(late_in, {"depth": place(lax.rem(lax.div(step, cores), rows_x), z_to, lax.rem(step, cores))})
             return carry
 
-        lax.fori_loop(0, EARLY * rows_x * cores, report, 0)
-
-    loads[2].wait()
+        lax.fori_loop(0, n_early, report, 0)
+
+    loads[4].wait()
     tab[0:4, 0:classes] = table_v[...]
-    loads[1].wait()
+    loads[3].wait()
 
     lane = lax.broadcasted_iota(jnp.int32, (SUB, LANES), 1)
     zero = jnp.zeros((SUB, LANES), F32)
@@ -158,8 +174,8 @@
 
     def shear_of(p):
         scaled = 3 * (me * planes + p)
-        offset = scaled // 8
-        fraction = (scaled % 8).astype(F32) * 0.125
+        offset = lax.div(scaled, 8)
+        fraction = lax.rem(scaled, 8).astype(F32) * 0.125
         return offset, fraction
 
     def look_up(p, carry):
@@ -214,20 +230,23 @@
 
     lax.fori_loop(0, planes, plane_terms, 0)
 
-    def fill(present, copy, slot, p):
+    def fill(present, copies, slot, p, piece):
+        span = range(pieces[piece].start // LANES, pieces[piece].stop // LANES)
+
         @pl.when(present)
         def _():
-            copy.wait_recv()
-            for t in range(tiles):
+            copies[piece].wait_recv()
+            for t in span:
                 put(p, t, plane_in[slot, :, t * LANES : (t + 1) * LANES].astype(F32))
 
         @pl.when(jnp.logical_not(present))
         def _():
-            for t in range(tiles):
+            for t in span:
                 put(p, t, jnp.zeros((height, LANES), F32))
 
-    fill(has_below, to_over, 0, 0)
-    fill(has_over, to_below, 1, planes + 1)
+    def fill_piece(piece):
+        fill(has_below, to_over, 0, 0, piece)
+        fill(has_over, to_below, 1, planes + 1, piece)
 
     def border(present, copy, slot, row):
         @pl.when(present)
@@ -241,6 +260,7 @@
             for p in range(planes):
                 field[row_of(p + 1, row), :] = jnp.zeros((tiles, LANES), F32)
 
+    fill_piece(0)
     border(has_upper, to_lower, 0, -1)
     border(has_lower, to_upper, 1, height)
 
@@ -251,13 +271,10 @@
         )
 
     def send(z_to, carry):
-        for step in range(rows_x):
-            for core_to in range(cores):
-                owner = place(lax.rem(x + step, rows_x), z_to, core_to)
-                if step == 0:
-                    pl.when(owner != me)(lambda owner=owner: tile_copy(owner).start())
-                else:
-                    tile_copy(owner).start()
+        for x_to in range(rows_x):
+            for core_to in reversed(range(cores)):
+                owner = place(x_to, z_to, core_to)
+                pl.when(owner != me)(tile_copy(owner).start)
         return carry
 
     shears = [shear_of(p) for p in range(planes)]
@@ -289,26 +306,43 @@
                     start = spot // per_owner * rows_msg + spot % per_owner
                     for c, value in enumerate(colour + [depth[h, t]]):
                         wide[pl.ds(start + c * per_owner, SUB, stride=tiles * 4), :] = value
-        for owner in range(bricks):
-            first_tile = owner * per_owner % tiles
-            if low <= first_tile < high:
-                packed[owner] = wide[owner * rows_msg : (owner + 1) * rows_msg, :].astype(jnp.bfloat16)
-
+
+    def pack(owners):
+        for owner in owners:
+            packed[owner] = wide[owner * rows_msg : (owner + 1) * rows_msg, :].astype(jnp.bfloat16)
+
+    def in_ring(owner):
+        return owner // cores % deep
+
+    everyone_else = [owner for owner in range(bricks) if in_ring(owner) != 0]
     if split:
         shade(0, split)
-        send(0, 0)
+    else:
+        fill_piece(1)
+        shade(0, tiles)
+    pack([owner for owner in range(bricks) if in_ring(owner) == 0])
+    send(0, 0)
+    if split:
+        fill_piece(1)
         shade(split, tiles)
-    else:
-        shade(0, tiles)
-        send(0, 0)
+    pack(everyone_else)
     lax.fori_loop(1, EARLY, send, 0)
+    for core_to in range(cores):
+        owner = place(0, EARLY, core_to)
+        pl.when(owner != me)(tile_copy(owner).start)
 
     @pl.when(early)
     def _():
-        pl.semaphore_wait(late_in, (deep - EARLY) * rows_x * cores)
-        for source, targets in RELAYS:
-
-            @pl.when(z == source)
+        pl.semaphore_wait(late_in, bricks - n_early)
+        wide_row = x == 0
+        thin_row = x > 0
+        for chosen, targets in (
+            (z == 0, (deep - 1, deep - 2)),
+            (jnp.logical_and(thin_row, z == EARLY - 1), (EARLY, EARLY + 1, EARLY + 2)),
+            (jnp.logical_and(wide_row, z == EARLY), (EARLY + 1, EARLY + 2)),
+        ):
+
+            @pl.when(chosen)
             def _(targets=targets):
                 for target in targets:
                     signal(all_in, {"depth": place(x, target, core)})
@@ -317,13 +351,18 @@
     def _():
         pl.semaphore_wait(all_in, 1)
 
-    lax.fori_loop(EARLY, deep, send, 0)
+    for step in range(1, rows_x):
+        for core_to in range(cores):
+            owner = place(step, EARLY, core_to)
+            pl.when(owner != me)(tile_copy(owner).start)
+    lax.fori_loop(EARLY + 1, deep, send, 0)
 
     own = pltpu.make_async_copy(packed.at[me], arrived.at[me], own_sem)
     own.start()
     own.wait()
-    pl.when(has_over)(to_over.wait_send)
-    pl.when(has_below)(to_below.wait_send)
+    for piece in range(2):
+        pl.when(has_over)(to_over[piece].wait_send)
+        pl.when(has_below)(to_below[piece].wait_send)
     pl.when(has_lower)(to_lower.wait_send)
     pl.when(has_upper)(to_upper.wait_send)
     everyone = pltpu.make_async_remote_copy(
@@ -341,10 +380,12 @@
     row = lax.broadcasted_iota(jnp.int32, (rows_msg, LANES), 0)
     last = row >= 3 * per_owner
 
+    group = min(bricks, 32)
+
     def layer(slot, carry):
         shown, prefix = carry
-        for inner in range(8):
-            tile = arrived[order[0, slot * 8 + inner]].astype(F32)
+        for inner in range(group):
+            tile = arrived[order[0, slot * group + inner]].astype(F32)
             shown = shown + jnp.exp(-prefix) * tile
             spread = jnp.where(last, tile, 0.0)
             spread = spread + pltpu.roll(spread, 2 * per_owner, 0)
@@ -353,7 +394,7 @@
         return shown, prefix
 
     blank = jnp.zeros((rows_msg, LANES), F32)
-    shown, prefix = lax.fori_loop(0, bricks // 8, layer, (blank, blank))
+    shown, prefix = lax.fori_loop(0, bricks // group, layer, (blank, blank))
     shown = jnp.where(last, jnp.exp(-prefix), shown)
     for r in range(rows_msg):
         c, piece = r // per_owner, r % per_owner
@@ -393,10 +434,10 @@
                 pltpu.VMEM((halves, tiles, SUB, LANES), F32),
                 pltpu.VMEM((bricks * rows_msg, LANES), F32),
                 pltpu.VMEM((bricks, rows_msg, LANES), jnp.bfloat16),
-                pltpu.SemaphoreType.DMA((3,)),
+                pltpu.SemaphoreType.DMA((5,)),
                 pltpu.SemaphoreType.DMA,
-                pltpu.SemaphoreType.DMA((4,)),
-                pltpu.SemaphoreType.DMA((4,)),
+                pltpu.SemaphoreType.DMA((6,)),
+                pltpu.SemaphoreType.DMA((6,)),
                 pltpu.SemaphoreType.DMA,
                 pltpu.SemaphoreType.DMA,
                 pltpu.SemaphoreType.REGULAR,

time: 19.9 us -> 19.1 us (0.960)
  Pallas kernels: 19.8 us -> 19 us
    pallas_call x1, Pallas kernels: 18 us -> 17.4 us  [per_device(): pl.pallas_call(functools.partial(kernel, bricks, strips, planes, height,...]
where the time goes in v4:
time: 19.1 us; the launch traced here: 19 us
  Pallas kernels  19 us (99%)
    pallas_call x1, Pallas kernels, per_device(): pl.pallas_call(functools.partial(kernel, bricks, strips, planes, height,...  17.4 us
    pallas_call x1, Pallas kernels, per_device(): pl.pallas_call(functools.partial(composite, bricks, rows_msg // 4), out_s...  1.65 us

profile of v4, /device:TPU:1, one launch (start us, length us, event | category | flops | bytes accessed | tf_op | source)
XLA Modules:
  0.0 19.0 jit_solution(12435144248621029520)
XLA Ops:
  0.0 17.4 %shard_map.46.arrived = bf16[64,8,128]{2,1,0:T(8,128)(2,1)} custom-call(bf16[4,16,1024]{2,1,0:T(8,128)(2,1)} %dens_hbm.1, s32[4,16,1024]{2,1,0:T(8,128)} %bins_hbm.1, f32[4,16]{1,0:T(4,128)} %table_hbm.1), custom_call_target="tpu_custom_call" | custom-call | tf_op jit(solution)/shard_map/pallas_call | solution.py:415
  17.4 1.6 %shard_map.47 = f32[4,256]{1,0:T(4,128)} custom-call(s32[1,64]{1,0:T(1,128)} %order.1, bf16[64,8,128]{2,1,0:T(8,128)(2,1)} %shard_map.46.arrived), custom_call_target="tpu_custom_call" | custom-call | tf_op jit(solution)/shard_map/pallas_call | solution.py:448

commit v5 on v4

--- a/solution.py
+++ b/solution.py
@@ -126,17 +126,21 @@
         )
 
     cut = (tiles // 2 + 1) * LANES
-    pieces = (slice(0, cut), slice(cut, across))
+    pieces = (
+        (slice(0, SUB), slice(0, cut)),
+        (slice(SUB, height), slice(0, cut)),
+        (slice(0, height), slice(cut, across)),
+    )
     to_over = [
-        halo(dens_v.at[planes - 1, :, part], plane_in.at[0, :, part], i, {"depth": over})
+        halo(dens_v.at[planes - 1, *part], plane_in.at[0, *part], i, {"depth": over})
         for i, part in enumerate(pieces)
     ]
     to_below = [
-        halo(dens_v.at[0, :, part], plane_in.at[1, :, part], 2 + i, {"depth": below})
+        halo(dens_v.at[0, *part], plane_in.at[1, *part], 3 + i, {"depth": below})
         for i, part in enumerate(pieces)
     ]
-    to_lower = halo(rows_out.at[1], rows_in.at[0], 4, {"strip": lax.rem(strip + 1, strips)})
-    to_upper = halo(rows_out.at[0], rows_in.at[1], 5, {"strip": lax.rem(strip + strips - 1, strips)})
+    to_lower = halo(rows_out.at[1], rows_in.at[0], 6, {"strip": lax.rem(strip + 1, strips)})
+    to_upper = halo(rows_out.at[0], rows_in.at[1], 7, {"strip": lax.rem(strip + strips - 1, strips)})
 
     loads[0].wait()
     loads[1].wait()
@@ -150,7 +154,7 @@
     pl.semaphore_wait(barrier, greeted)
     pl.when(has_lower)(to_lower.start)
     pl.when(has_upper)(to_upper.start)
-    for piece in range(2):
+    for piece in range(len(pieces)):
         pl.when(has_over)(to_over[piece].start)
         pl.when(has_below)(to_below[piece].start)
 
@@ -231,18 +235,22 @@
     lax.fori_loop(0, planes, plane_terms, 0)
 
     def fill(present, copies, slot, p, piece):
-        span = range(pieces[piece].start // LANES, pieces[piece].stop // LANES)
+        rows, columns = pieces[piece]
+        span = range(columns.start // LANES, columns.stop // LANES)
+        count = rows.stop - rows.start
 
         @pl.when(present)
         def _():
             copies[piece].wait_recv()
             for t in span:
-                put(p, t, plane_in[slot, :, t * LANES : (t + 1) * LANES].astype(F32))
+                field[at(p, t, rows.start, count), :] = plane_in[
+                    slot, rows, t * LANES : (t + 1) * LANES
+                ].astype(F32)
 
         @pl.when(jnp.logical_not(present))
         def _():
             for t in span:
-                put(p, t, jnp.zeros((height, LANES), F32))
+                field[at(p, t, rows.start, count), :] = jnp.zeros((count, LANES), F32)
 
     def fill_piece(piece):
         fill(has_below, to_over, 0, 0, piece)
@@ -260,9 +268,6 @@
             for p in range(planes):
                 field[row_of(p + 1, row), :] = jnp.zeros((tiles, LANES), F32)
 
-    fill_piece(0)
-    border(has_upper, to_lower, 0, -1)
-    border(has_lower, to_upper, 1, height)
 
     def tile_copy(owner):
         return pltpu.make_async_remote_copy(
@@ -280,8 +285,8 @@
     shears = [shear_of(p) for p in range(planes)]
     split = tiles // 2 if 4 * per_owner == tiles else 0
 
-    def shade(low, high):
-        for h in range(halves):
+    def shade(low, high, chosen):
+        for h in chosen:
             before = [(zero, zero)] * planes
             for t in reversed(range(low, min(high + 1, tiles))):
                 colour = [zero] * 3
@@ -314,18 +319,39 @@
     def in_ring(owner):
         return owner // cores % deep
 
-    everyone_else = [owner for owner in range(bricks) if in_ring(owner) != 0]
+    def first_owners(spot):
+        return [
+            place(x_to, 0, core_to)
+            for x_to in range(rows_x)
+            for core_to in reversed(range(cores))
+            if place(x_to, 0, core_to) * per_owner // (SUB * tiles) == spot
+        ]
+
+    def send_first(spot):
+        pack(first_owners(spot))
+        for owner in first_owners(spot):
+            pl.when(owner != me)(tile_copy(owner).start)
+
     if split:
-        shade(0, split)
+        fill_piece(0)
+        border(has_upper, to_lower, 0, -1)
+        shade(0, split, (0,))
+        send_first(0)
+        fill_piece(1)
+        border(has_lower, to_upper, 1, height)
+        shade(0, split, (1,))
+        send_first(1)
+        fill_piece(2)
+        shade(split, tiles, range(halves))
     else:
-        fill_piece(1)
-        shade(0, tiles)
-    pack([owner for owner in range(bricks) if in_ring(owner) == 0])
-    send(0, 0)
-    if split:
-        fill_piece(1)
-        shade(split, tiles)
-    pack(everyone_else)
+        for piece in range(len(pieces)):
+            fill_piece(piece)
+        border(has_upper, to_lower, 0, -1)
+        border(has_lower, to_upper, 1, height)
+        shade(0, tiles, range(halves))
+        send_first(0)
+        send_first(1)
+    pack([owner for owner in range(bricks) if in_ring(owner) != 0])
     lax.fori_loop(1, EARLY, send, 0)
     for core_to in range(cores):
         owner = place(0, EARLY, core_to)
@@ -360,7 +386,7 @@
     own = pltpu.make_async_copy(packed.at[me], arrived.at[me], own_sem)
     own.start()
     own.wait()
-    for piece in range(2):
+    for piece in range(len(pieces)):
         pl.when(has_over)(to_over[piece].wait_send)
         pl.when(has_below)(to_below[piece].wait_send)
     pl.when(has_lower)(to_lower.wait_send)
@@ -436,8 +462,8 @@
                 pltpu.VMEM((bricks, rows_msg, LANES), jnp.bfloat16),
                 pltpu.SemaphoreType.DMA((5,)),
                 pltpu.SemaphoreType.DMA,
-                pltpu.SemaphoreType.DMA((6,)),
-                pltpu.SemaphoreType.DMA((6,)),
+                pltpu.SemaphoreType.DMA((8,)),
+                pltpu.SemaphoreType.DMA((8,)),
                 pltpu.SemaphoreType.DMA,
                 pltpu.SemaphoreType.DMA,
                 pltpu.SemaphoreType.REGULAR,

time: 19.1 us -> 18.6 us (0.974)
  Pallas kernels: 19 us -> 18.5 us
    pallas_call x1, Pallas kernels: 17.4 us -> 16.9 us  [per_device(): pl.pallas_call(functools.partial(kernel, bricks, strips, planes, height,...]
where the time goes in v5:
time: 18.6 us; the launch traced here: 18.5 us
  Pallas kernels  18.5 us (99%)
    pallas_call x1, Pallas kernels, per_device(): pl.pallas_call(functools.partial(kernel, bricks, strips, planes, height,...  16.9 us
    pallas_call x1, Pallas kernels, per_device(): pl.pallas_call(functools.partial(composite, bricks, rows_msg // 4), out_s...  1.65 us

profile of v5, /device:TPU:1, one launch (start us, length us, event | category | flops | bytes accessed | tf_op | source)
XLA Modules:
  0.0 18.5 jit_solution(11963065735759683730)
XLA Ops:
  0.0 16.9 %shard_map.46.arrived = bf16[64,8,128]{2,1,0:T(8,128)(2,1)} custom-call(bf16[4,16,1024]{2,1,0:T(8,128)(2,1)} %dens_hbm.1, s32[4,16,1024]{2,1,0:T(8,128)} %bins_hbm.1, f32[4,16]{1,0:T(4,128)} %table_hbm.1), custom_call_target="tpu_custom_call" | custom-call | tf_op jit(solution)/shard_map/pallas_call | solution.py:441
  16.9 1.6 %shard_map.47 = f32[4,256]{1,0:T(4,128)} custom-call(s32[1,64]{1,0:T(1,128)} %order.1, bf16[64,8,128]{2,1,0:T(8,128)(2,1)} %shard_map.46.arrived), custom_call_target="tpu_custom_call" | custom-call | tf_op jit(solution)/shard_map/pallas_call | solution.py:474

commit v6 on v5

--- a/solution.py
+++ b/solution.py
@@ -81,7 +81,7 @@
         pltpu.make_async_copy(bins_hbm, bins_v, in_sem.at[3]),
         pltpu.make_async_copy(table_hbm, table_v, in_sem.at[4]),
     ]
-    for load in loads:
+    for load in loads[:3]:
         load.start()
 
     barrier = pltpu.get_barrier_semaphore()
@@ -145,6 +145,8 @@
     loads[0].wait()
     loads[1].wait()
     loads[2].wait()
+    for load in loads[3:]:
+        load.start()
     for p in range(planes):
         for t in range(tiles):
             put(p + 1, t, dens_v[p, :, t * LANES : (t + 1) * LANES].astype(F32))
@@ -327,16 +329,19 @@
             if place(x_to, 0, core_to) * per_owner // (SUB * tiles) == spot
         ]
 
-    def send_first(spot):
-        pack(first_owners(spot))
-        for owner in first_owners(spot):
+    def send_first(spot, which=(1, 0)):
+        chosen = [owner for core_to in which for owner in first_owners(spot) if owner % cores == core_to]
+        pack(chosen)
+        for owner in chosen:
             pl.when(owner != me)(tile_copy(owner).start)
 
     if split:
         fill_piece(0)
         border(has_upper, to_lower, 0, -1)
-        shade(0, split, (0,))
-        send_first(0)
+        shade(split // 2, split, (0,))
+        send_first(0, (1,))
+        shade(0, split // 2, (0,))
+        send_first(0, (0,))
         fill_piece(1)
         border(has_lower, to_upper, 1, height)
         shade(0, split, (1,))

time: 18.6 us -> 18.7 us (level)
  no operation moved by 1% of the time
where the time goes in v6:
time: 18.7 us; the launch traced here: 18.5 us
  Pallas kernels  18.5 us (99%)
    pallas_call x1, Pallas kernels, per_device(): pl.pallas_call(functools.partial(kernel, bricks, strips, planes, height,...  16.9 us
    pallas_call x1, Pallas kernels, per_device(): pl.pallas_call(functools.partial(composite, bricks, rows_msg // 4), out_s...  1.65 us

profile of v6, /device:TPU:1, one launch (start us, length us, event | category | flops | bytes accessed | tf_op | source)
XLA Modules:
  0.0 18.5 jit_solution(10146009422415092411)
XLA Ops:
  0.0 16.9 %shard_map.46.arrived = bf16[64,8,128]{2,1,0:T(8,128)(2,1)} custom-call(bf16[4,16,1024]{2,1,0:T(8,128)(2,1)} %dens_hbm.1, s32[4,16,1024]{2,1,0:T(8,128)} %bins_hbm.1, f32[4,16]{1,0:T(4,128)} %table_hbm.1), custom_call_target="tpu_custom_call" | custom-call | tf_op jit(solution)/shard_map/pallas_call | solution.py:446
  16.9 1.6 %shard_map.47 = f32[4,256]{1,0:T(4,128)} custom-call(s32[1,64]{1,0:T(1,128)} %order.1, bf16[64,8,128]{2,1,0:T(8,128)(2,1)} %shard_map.46.arrived), custom_call_target="tpu_custom_call" | custom-call | tf_op jit(solution)/shard_map/pallas_call | solution.py:479
